TPU v7x, 32 devices: a whole 2x2x4 slice. The times are simulated.
32 devices in a mesh: tile: 8 (over z, y), hidden: 4 (over x, core).
Axes of the slice: x: 2, y: 2, z: 4, core: 2. Of those that a mesh axis runs over, the one named last changes fastest.
Arguments:
- cells: bfloat16 [128, 48, 48, 128], P(('tile', 'hidden')), may hold values from -6 to 6
- partner_edge: int32 [128, 4], P(('tile', 'hidden')), may hold values from 0 to 511, as said below
- edge_flip: int32 [128, 4], P(('tile', 'hidden')), may hold values from 0 to 1, as said below
- dw_weight: float32 [9, 128], replicated, may hold values from -2 to 2
- dw_bias: float32 [128], replicated, may hold values from -3 to 3
- ln_gain: float32 [128], replicated, may hold values from 0.5 to 1.5
- ln_bias: float32 [128], replicated, may hold values from -3 to 3
- w_in: bfloat16 [512, 128], replicated, may hold values from -0.5 to 0.5
- b_in: bfloat16 [512], replicated, may hold values from -3 to 3
- w_out: bfloat16 [512, 128], replicated, may hold values from -0.25 to 0.25
- b_out: float32 [128], replicated, may hold values from -3 to 3
- layer_scale: float32 [128], replicated, may hold values from 0.5 to 1.5
Outputs:
- updated: bfloat16 [128, 48, 48, 128], P(('tile', 'hidden'))
Inputs may be any that keep to these rules, and one draw needn't show every extreme that they name: `partner_edge`: edges are matched in pairs: if edge a names edge b, then b names a, a != b, and both carry the same edge_flip. Every edge's partner lies on the same device as its tile or on the device just before or just after it in the order of tile+hidden, the last and the first being neighbours; exactly 4 edges of each device have partners on the next device. `edge_flip`: equal at the two edges of a matched pair.
All inputs are finite; a program needn't handle non-finite values.
Results may differ from a plain program's by a relative error of at most 0.0044.
Values may be sent and summed in bfloat16 or wider, within the bound.
A program may use at most 64 MiB of HBM per device.

v0:
```python
import jax
import jax.numpy as jnp
from jax import lax
from jax.sharding import PartitionSpec as P


def shifted(array, axis, by):
    count = lax.axis_size(axis)
    return lax.ppermute(array, axis, [(i, (i + by) % count) for i in range(count)])


def boundary(tiles_in):
    return jnp.stack(
        [tiles_in[:, 0], tiles_in[:, :, -1], tiles_in[:, -1], tiles_in[:, :, 0]], axis=1
    )


def pad_tiles(tiles_in, halo_rows):
    north_rim = halo_rows[:, 0].astype(jnp.float32)
    east_rim = halo_rows[:, 1].astype(jnp.float32)
    south_rim = halo_rows[:, 2].astype(jnp.float32)
    west_rim = halo_rows[:, 3].astype(jnp.float32)
    top_row = jnp.concatenate(
        [
            0.5 * (north_rim[:, :1] + west_rim[:, :1]),
            north_rim,
            0.5 * (north_rim[:, -1:] + east_rim[:, :1]),
        ],
        axis=1,
    )
    bottom_row = jnp.concatenate(
        [
            0.5 * (south_rim[:, :1] + west_rim[:, -1:]),
            south_rim,
            0.5 * (south_rim[:, -1:] + east_rim[:, -1:]),
        ],
        axis=1,
    )
    middle = jnp.concatenate(
        [west_rim[:, :, None], tiles_in.astype(jnp.float32), east_rim[:, :, None]], axis=2
    )
    return jnp.concatenate([top_row[:, None], middle, bottom_row[:, None]], axis=1)


def depthwise(padded, dw_weight, dw_bias):
    side_len = padded.shape[1] - 2
    total = jnp.zeros(padded[:, 1:-1, 1:-1].shape, jnp.float32) + dw_bias
    for row_tap in range(3):
        for col_tap in range(3):
            total = (
                total
                + dw_weight[3 * row_tap + col_tap]
                * padded[:, row_tap : row_tap + side_len, col_tap : col_tap + side_len]
            )
    return total


def layer_norm(conv, ln_gain, ln_bias):
    center = jnp.mean(conv, axis=-1, keepdims=True)
    spread = jnp.mean((conv - center) ** 2, axis=-1, keepdims=True)
    return ((conv - center) * lax.rsqrt(spread + 1e-06) * ln_gain + ln_bias).astype(jnp.bfloat16)


def per_device(
    cells,
    partner_edge,
    edge_flip,
    dw_weight,
    dw_bias,
    ln_gain,
    ln_bias,
    w_in,
    b_in,
    w_out,
    b_out,
    layer_scale,
):
    tile_count, tile_side, _, channels = cells.shape
    edge_count = 4 * tile_count
    boundary_rows = boundary(cells).reshape(edge_count, tile_side, channels)
    devices = lax.axis_size(("tile", "hidden"))
    position = lax.axis_index(("tile", "hidden"))
    flat_partner = partner_edge.reshape(edge_count)
    flat_flip = edge_flip.reshape(edge_count)
    owner_device = flat_partner // edge_count
    local_edge = flat_partner % edge_count
    distance = jnp.mod(owner_device - position, devices)
    from_prev = distance == devices - 1
    from_next = distance == 1
    before = shifted(boundary_rows, ("tile", "hidden"), 1)
    after = shifted(boundary_rows, ("tile", "hidden"), -1)
    candidates = jnp.concatenate([before, boundary_rows, after], axis=0)
    pick_index = jnp.where(
        from_prev,
        local_edge,
        jnp.where(from_next, 2 * edge_count + local_edge, edge_count + local_edge),
    )
    halo_rows = candidates[pick_index]
    halo_rows = jnp.where(flat_flip[:, None, None] == 1, halo_rows[:, ::-1], halo_rows)
    halo_rows = halo_rows.reshape(tile_count, 4, tile_side, channels)
    padded = pad_tiles(cells, halo_rows)
    conv = depthwise(padded, dw_weight, dw_bias)
    normed = layer_norm(conv, ln_gain, ln_bias).reshape(-1, channels)
    pre = lax.dot_general(
        normed, w_in, (((1,), (1,)), ((), ())), preferred_element_type=jnp.float32
    ) + b_in.astype(jnp.float32)
    act = jax.nn.gelu(pre, approximate=False).astype(jnp.bfloat16)
    mixed = jnp.dot(act, w_out, preferred_element_type=jnp.float32) + b_out
    mixed = mixed.reshape(tile_count, tile_side, tile_side, channels)
    return (cells.astype(jnp.float32) + layer_scale * mixed).astype(jnp.bfloat16)


def solution(mesh):
    in_specs = (
        P(("tile", "hidden"), None, None, None),
        P(("tile", "hidden"), None),
        P(("tile", "hidden"), None),
        P(),
        P(),
        P(),
        P(),
        P(),
        P(),
        P(),
        P(),
        P(),
    )
    out_specs = P(("tile", "hidden"), None, None, None)
    return jax.shard_map(
        per_device, mesh=mesh, in_specs=in_specs, out_specs=out_specs, check_vma=False
    )
```

profile of v0, /device:TPU:0, one launch (start us, length us, event | category | flops | bytes accessed | tf_op | source)
XLA Modules:
  0.0 87.3 jit_solution(13249152883240855540)
XLA Ops:
  0.0 0.0 copy-start
  0.0 1.3 %fusion.65 = (bf16[4,48,1,128]{3,2,1,0:T(2,128)(2,1)S(1)}, bf16[4,48,1,128]{3,2,1,0:T(2,128)(2,1)S(1)}) fusion(bf16[4,48,48,128]{3,2,1,0:T(8,128)(2,1)} %param.12), kind=kLoop, calls=%fused_computation.129 | loop fusion | bytes 196608 | tf_op jit(solution)/shard_map/slice | solution.py:14
  1.3 0.8 slice_bitcast_fusion.5
  2.2 0.5 collective-permute-start
  2.8 6.0 %collective-permute-start.1 = (bf16[16,48,128]{2,1,0:T(8,128)(2,1)S(1)}, bf16[16,48,128]{2,1,0:T(8,128)(2,1)S(1)}, u32[]{:S(2)}, u32[]{:S(2)}) collective-permute-start(bf16[16,48,128]{2,1,0:T(8,128)(2,1)S(1)} %bitcast.96), channel_id=1, source_target_pairs={{0,31},{1,0},{2,1},{3,2},{4,3},{5,4},{6,5},{7,6},{8,7},{9,8},{10,9... | collective-permute-start | bytes 589832 | tf_op jit(solution)/shard_map/ppermute | solution.py:9
  8.8 4.2 %convert_element_type.64 = f32[4,48,48,128]{3,2,1,0:T(8,128)} convert(bf16[4,48,48,128]{3,2,1,0:T(8,128)(2,1)} %param.12) | non-fusion elementwise | flops 1179648 | bytes 7077888 | tf_op jit(solution)/shard_map/convert_element_type | solution.py:110
  12.9 0.8 reshape.242
  13.8 0.7 broadcast_compare_fusion
  14.4 0.1 eq.35
  14.5 1.3 %convert_element_type.78 = f32[512]{0:T(512)} convert(bf16[512]{0:T(512)(128)(2,1)} %param.20) | non-fusion elementwise | flops 512 | bytes 3072 | tf_op jit(solution)/shard_map/convert_element_type | solution.py:106
  15.8 1.6 %slice_bitcast_fusion.14 = (f32[128]{0:T(128)S(1)}, f32[128]{0:T(128)S(1)}, f32[128]{0:T(128)}, f32[128]{0:T(128)}, f32[128]{0:T(128)}, /*index=5*/f32[128]{0:T(128)}, f32[128]{0:T(128)}, f32[128]{0:T(128)}, f32[128]{0:T(128)}) fusion(f32[9,128]{1,0:T(8,128)} %param.15), kind=kLoop, calls=%fused_computation.97 | loop fusion | bytes 9216 | tf_op jit(solution)/shard_map/mul | solution.py:52
  17.4 0.0 collective-permute-done
  17.4 0.0 collective-permute-done.1
  17.4 0.1 pad_maximum_fusion.3
  17.5 0.0 slice-start
  17.5 0.6 gather_fusion
  18.1 0.1 rev.3
  18.2 0.1 broadcast_select_fusion
  18.4 0.0 slice-start.1
  18.4 5.0 %maximum_maximum_fusion = (f32[4,49,50,128]{3,2,1,0:T(8,128)S(1)}, f32[4,49,50,128]{3,2,1,0:T(8,128)S(1)}) fusion(f32[4,48,1,128]{3,2,1,0:T(1,128)S(1)} %bitcast.93, f32[4,48,48,128]{3,2,1,0:T(8,128)} %convert_element_type.64, f32[4,48,1,128]{3,2,1,0:T(1,128)S(1)} %bitcast.91, f32[4,1,50,128]{3,2,1,0:T(8,128)S(1)} %maximum_bitcast_fusion, ...), kind=kLoop, calls=%fused_computation.21 | loop fusion | flops 7526400 | bytes 15155200 | tf_op jit(solution)/shard_map/concatenate | solution.py:42
  23.4 0.0 slice-done
  23.4 0.0 slice-done.1
  23.4 7.0 %fusion.63 = (f32[4,48,48]{2,1,0:T(8,128)}, f32[4,48,48,128]{3,2,1,0:T(8,128)S(1)}) fusion(f32[4,49,50,128]{3,2,1,0:T(8,128)S(1)} %get-tuple-element.8, f32[128]{0:T(128)} %get-tuple-element.30, f32[128]{0:T(128)} %get-tuple-element.31, f32[128]{0:T(128)S(1)} %get-tuple-element.24, f32[4,48,1,128]{3,2,1,0:T(1,128)S(1)} %bitcast.94, ...), kind=kLoop, calls=%fused_computation.128 | loop fusion | flops 24763392 | bytes 37987328 | tf_op jit(solution)/shard_map/reduce_sum | solution.py:59
  30.4 0.0 copy-start.4
  30.4 0.9 %broadcast_multiply_fusion = f32[4,48,48]{2,1,0:T(8,128)S(1)} fusion(f32[4,48,48]{2,1,0:T(8,128)} %get-tuple-element.5), kind=kLoop, calls=%fused_computation.61 | loop fusion | flops 9216 | bytes 73728 | tf_op jit(solution)/shard_map/div | solution.py:59
  31.3 2.8 %multiply_reduce_fusion = f32[4,48,48]{2,1,0:T(8,128)S(1)} fusion(f32[4,48,48,128]{3,2,1,0:T(8,128)S(1)} %get-tuple-element.6, f32[4,48,48]{2,1,0:T(8,128)S(1)} %broadcast_multiply_fusion), kind=kLoop, calls=%fused_computation.44 | loop fusion | flops 3529728 | bytes 4792320 | tf_op jit(solution)/shard_map/reduce_sum | solution.py:60
  34.1 3.6 %add_convert_fusion.1 = bf16[4,48,48,128]{3,2,1,0:T(8,128)(2,1)S(1)} fusion(f32[4,48,48,128]{3,2,1,0:T(8,128)S(1)} %get-tuple-element.6, f32[128]{0:T(128)} %param.18, f32[128]{0:T(128)} %param.17, f32[4,48,48]{2,1,0:T(8,128)S(1)} %add_rsqrt_fusion, f32[4,48,48]{2,1,0:T(8,128)S(1)} %broadcast_multiply_fusion), kind=kLoop, calls=%fused_computation.43 | loop fusion | flops 5898240 | bytes 7152640 | tf_op jit(solution)/shard_map/convert_element_type | solution.py:61
  37.8 0.0 copy-done
  37.8 0.0 copy-done.4
  37.8 0.0 copy-start.2
  37.8 0.0 copy-start.3
  37.8 44.8 %fusion.2.clone.4 = bf16[9216,512]{1,0:T(8,128)(2,1)S(1)} fusion(bf16[9216,128]{1,0:T(8,128)(2,1)S(1)} %bitcast.90, bf16[512,128]{1,0:T(8,128)(2,1)S(1)} %copy-done, f32[512]{0:T(512)S(1)} %copy-done.4), kind=kOutput, calls=%fused_computation.4.clone.clone.clone.1 | convolution fusion | flops 1519386624 | bytes 11929600 | tf_op jit(solution)/shard_map/dot_general | solution.py:104
  82.6 0.0 copy-done.2
  82.6 0.0 copy-done.3
  82.6 0.0 copy-start.1
  82.6 0.0 copy-start.5
  82.6 2.6 %convolution_add_fusion = f32[9216,128]{1,0:T(8,128)S(1)} fusion(bf16[512,128]{1,0:T(8,128)(2,1)S(1)} %copy-done.2, f32[128]{0:T(128)S(1)} %copy-done.3, bf16[9216,512]{1,0:T(8,128)(2,1)S(1)} %fusion.2.clone.4), kind=kOutput, calls=%fused_computation.20 | convolution fusion | flops 1209139200 | bytes 14287360 | tf_op jit(solution)/shard_map/dot_general | solution.py:108
  85.3 0.0 copy-done.1
  85.3 0.0 copy-done.5
  85.3 2.0 %add_convert_fusion = bf16[4,48,48,128]{3,2,1,0:T(8,128)(2,1)} fusion(f32[4,48,48,128]{3,2,1,0:T(8,128)S(1)} %bitcast.89, f32[128]{0:T(128)S(1)} %copy-done.5, bf16[4,48,48,128]{3,2,1,0:T(8,128)(2,1)S(1)} %copy-done.1), kind=kLoop, calls=%fused_computation.42 | loop fusion | flops 4718592 | bytes 9437696 | tf_op jit(solution)/shard_map/convert_element_type | solution.py:110
  (11 shorter events, 0.2 us)
Async XLA Ops:
  0.0 37.8 %copy-start = (bf16[512,128]{1,0:T(8,128)(2,1)S(1)}, bf16[512,128]{1,0:T(8,128)(2,1)}, u32[]{:S(2)}) copy-start(bf16[512,128]{1,0:T(8,128)(2,1)} %param.19) | copy-start | bytes 393220
  2.2 15.1 %collective-permute-start = (bf16[16,48,128]{2,1,0:T(8,128)(2,1)S(1)}, bf16[16,48,128]{2,1,0:T(8,128)(2,1)S(1)}, u32[]{:S(2)}, u32[]{:S(2)}) collective-permute-start(bf16[16,48,128]{2,1,0:T(8,128)(2,1)S(1)} %bitcast.95), channel_id=1, source_target_pairs={{0,1},{1,2},{2,3},{3,4},{4,5},{5,6},{6,7},{7,8},{8,9},{9,10},{10,1... | collective-permute-start | bytes 589832 | tf_op jit(solution)/shard_map/ppermute | solution.py:9
  2.8 14.6 %collective-permute-start.1 = (bf16[16,48,128]{2,1,0:T(8,128)(2,1)S(1)}, bf16[16,48,128]{2,1,0:T(8,128)(2,1)S(1)}, u32[]{:S(2)}, u32[]{:S(2)}) collective-permute-start(bf16[16,48,128]{2,1,0:T(8,128)(2,1)S(1)} %bitcast.96), channel_id=1, source_target_pairs={{0,31},{1,0},{2,1},{3,2},{4,3},{5,4},{6,5},{7,6},{8,7},{9,8},{10,9... | collective-permute-start | bytes 589832 | tf_op jit(solution)/shard_map/ppermute | solution.py:9
  17.5 5.9 %slice-start = ((s8[4718592]{0:T(1024)(128)(4,1)}), s8[524288]{0:T(1024)(128)(4,1)S(1)}, s32[]{:S(2)}) async-start(s8[4718592]{0:T(1024)(128)(4,1)} %bitcast.87), calls=%async_computation | async-start | bytes 1048576
  18.4 5.0 %slice-start.1 = ((s8[4718592]{0:T(1024)(128)(4,1)}), s8[4194304]{0:T(1024)(128)(4,1)S(1)}, s32[]{:S(2)}) async-start(s8[4718592]{0:T(1024)(128)(4,1)} %bitcast.87), calls=%async_computation.1 | async-start | bytes 8388608
  30.4 7.4 %copy-start.4 = (f32[512]{0:T(512)S(1)}, f32[512]{0:T(512)}, u32[]{:S(2)}) copy-start(f32[512]{0:T(512)} %convert_element_type.78) | copy-start | bytes 6148
  37.8 44.8 %copy-start.2 = (bf16[512,128]{1,0:T(8,128)(2,1)S(1)}, bf16[512,128]{1,0:T(8,128)(2,1)}, u32[]{:S(2)}) copy-start(bf16[512,128]{1,0:T(8,128)(2,1)} %param.21) | copy-start | bytes 393220
  37.8 44.8 %copy-start.3 = (f32[128]{0:T(128)S(1)}, f32[128]{0:T(128)}, u32[]{:S(2)}) copy-start(f32[128]{0:T(128)} %param.22) | copy-start | bytes 1540
  82.6 2.6 %copy-start.1 = (bf16[4,48,48,128]{3,2,1,0:T(8,128)(2,1)S(1)}, bf16[4,48,48,128]{3,2,1,0:T(8,128)(2,1)}, u32[]{:S(2)}) copy-start(bf16[4,48,48,128]{3,2,1,0:T(8,128)(2,1)} %param.12) | copy-start | bytes 7077892
  82.6 2.6 %copy-start.5 = (f32[128]{0:T(128)S(1)}, f32[128]{0:T(128)}, u32[]{:S(2)}) copy-start(f32[128]{0:T(128)} %param.23) | copy-start | bytes 1540
where the time goes:
time: 87.7 us; the launch traced here: 87.3 us
  matrix products  47.4 us (54%)
  other arithmetic  27.8 us (32%)
  starting transfers between devices  6.52 us (7%)
  local copies, waits for them, and re-layouts  5.33 us (6%)
    dot_general x1, matrix products, per_device(): lax.dot_general(normed, w_in, (((1,), (1,)), ((), ())), preferred_element...  44.8 us
    reduce_sum x1, other arithmetic, layer_norm(): center = jnp.mean(conv, axis=-1, keepdims=True)  7.03 us
    ppermute x2, starting transfers between devices, shifted(): lax.ppermute(array, axis, [(i, (i + by) % count) for i in range(count)])  6.52 us
    concatenate x1, other arithmetic, pad_tiles(): jnp.concatenate([top_row[:, None], middle, bottom_row[:, None]], axis=1)  4.97 us
    convert_element_type x1, other arithmetic, per_device(): cells.astype(jnp.float32) + layer_scale * mixed  4.19 us
    convert_element_type x1, other arithmetic, layer_norm(): ((conv - center) * lax.rsqrt(spread + 1e-06) * ln_gain + ln_bias).astype(...  3.65 us
    reduce_sum x1, other arithmetic, layer_norm(): spread = jnp.mean((conv - center) ** 2, axis=-1, keepdims=True)  2.76 us
    dot_general x1, matrix products, per_device(): mixed = jnp.dot(act, w_out, preferred_element_type=jnp.float32) + b_out  2.61 us
  transfers between devices with their start and end apart: 2, of which 0 were waited for; matrix products, arithmetic and copies ran while one was open for 10% of the time, Pallas kernels for 0%

commit v1 on v0

v1 whole, which is shorter than its diff:
```python
import functools

import jax
import jax.numpy as jnp
from jax import lax
from jax.experimental import pallas as pl
from jax.experimental.pallas import tpu as pltpu
from jax.sharding import PartitionSpec as P

AXES = ("tile", "hidden")
OFF = 8


def shifted(array, by):
    count = lax.axis_size(AXES)
    return lax.ppermute(array, AXES, [(i, (i + by) % count) for i in range(count)])


def boundary(tiles_in):
    return jnp.stack(
        [tiles_in[:, 0], tiles_in[:, :, -1], tiles_in[:, -1], tiles_in[:, :, 0]], axis=1
    )


def block_kernel(
    rows,
    pick_ref,
    flip_ref,
    cells_ref,
    cand_ref,
    dw_ref,
    vec_ref,
    w_in_ref,
    b_in_ref,
    w_out_ref,
    out_ref,
    pad_ref,
):
    side = cells_ref.shape[1]
    channels = cells_ref.shape[3]
    tile = pl.program_id(0)
    pad_ref[pl.ds(1, side), pl.ds(OFF, side), :] = cells_ref[0].astype(jnp.float32)
    r_id = lax.broadcasted_iota(jnp.int32, (side, side), 0)
    c_id = lax.broadcasted_iota(jnp.int32, (side, side), 1)
    lines = []
    for s in range(4):
        edge = tile * 4 + s
        target = jnp.where(flip_ref[edge] == 1, side - 1 - r_id, r_id)
        order = jnp.where(c_id == target, 1.0, 0.0).astype(jnp.bfloat16)
        lines.append(
            jnp.dot(order, cand_ref[pick_ref[edge]], preferred_element_type=jnp.float32)
        )
    north, east, south, west = lines
    pad_ref[0, pl.ds(OFF, side), :] = north
    pad_ref[side + 1, pl.ds(OFF, side), :] = south
    for r in range(side):
        pad_ref[r + 1, OFF - 1 : OFF, :] = west[r : r + 1]
        pad_ref[r + 1, OFF + side : OFF + side + 1, :] = east[r : r + 1]
    pad_ref[0, OFF - 1 : OFF, :] = 0.5 * (north[:1] + west[:1])
    pad_ref[0, OFF + side : OFF + side + 1, :] = 0.5 * (north[-1:] + east[:1])
    pad_ref[side + 1, OFF - 1 : OFF, :] = 0.5 * (south[:1] + west[-1:])
    pad_ref[side + 1, OFF + side : OFF + side + 1, :] = 0.5 * (south[-1:] + east[-1:])

    dw_bias = vec_ref[0:1]
    gain = vec_ref[1:2]
    bias = vec_ref[2:3]
    b_out = vec_ref[3:4]
    scale = vec_ref[4:5]
    b_in = b_in_ref[...].astype(jnp.float32)

    @pl.loop(0, side // rows)
    def _(step):
        base = step * rows
        normed = []
        for r in range(rows):
            total = jnp.broadcast_to(dw_bias, (side, channels))
            for a in range(3):
                for b in range(3):
                    k = 3 * a + b
                    total = total + dw_ref[k : k + 1] * pad_ref[
                        base + r + a, pl.ds(OFF - 1 + b, side), :
                    ]
            center = total - jnp.mean(total, axis=-1, keepdims=True)
            spread = jnp.mean(center * center, axis=-1, keepdims=True)
            value = center * lax.rsqrt(spread + 1e-06) * gain + bias
            normed.append(value.astype(jnp.bfloat16))
        normed = jnp.concatenate(normed, axis=0)
        pre = (
            lax.dot_general(
                normed,
                w_in_ref[...],
                (((1,), (1,)), ((), ())),
                preferred_element_type=jnp.float32,
            )
            + b_in
        )
        half = 0.5 * pre
        act = (half + half * lax.erf(pre * 0.7071067811865476)).astype(jnp.bfloat16)
        mixed = jnp.dot(act, w_out_ref[...], preferred_element_type=jnp.float32) + b_out
        mixed = (scale * mixed).reshape(rows, side, channels)
        old = cells_ref[0, pl.ds(base, rows)].astype(jnp.float32)
        out_ref[0, pl.ds(base, rows)] = (old + mixed).astype(out_ref.dtype)


def per_device(
    cells,
    partner_edge,
    edge_flip,
    dw_weight,
    dw_bias,
    ln_gain,
    ln_bias,
    w_in,
    b_in,
    w_out,
    b_out,
    layer_scale,
):
    tile_count, side, _, channels = cells.shape
    hidden = w_in.shape[0]
    edge_count = 4 * tile_count
    rims = boundary(cells).reshape(edge_count, side, channels)
    devices = lax.axis_size(AXES)
    position = lax.axis_index(AXES)
    flat_partner = partner_edge.reshape(edge_count)
    flat_flip = edge_flip.reshape(edge_count)
    local_edge = flat_partner % edge_count
    distance = jnp.mod(flat_partner // edge_count - position, devices)
    group = jnp.where(distance == devices - 1, 0, jnp.where(distance == 1, 2, 1))
    pick = group * edge_count + local_edge
    before = shifted(rims, 1)
    after = shifted(rims, -1)
    cand = jnp.concatenate([before, rims, after], axis=0)
    vec = jnp.stack([dw_bias, ln_gain, ln_bias, b_out, layer_scale], axis=0)

    def whole(shape):
        return pl.BlockSpec(shape, lambda t, p, f: (0,) * len(shape))

    tile_spec = pl.BlockSpec((1, side, side, channels), lambda t, p, f: (t, 0, 0, 0))
    return pl.pallas_call(
        functools.partial(block_kernel, 4),
        out_shape=jax.ShapeDtypeStruct(cells.shape, jnp.bfloat16),
        grid_spec=pltpu.PrefetchScalarGridSpec(
            num_scalar_prefetch=2,
            grid=(tile_count,),
            in_specs=[
                tile_spec,
                whole(cand.shape),
                whole(dw_weight.shape),
                whole(vec.shape),
                whole(w_in.shape),
                whole((1, hidden)),
                whole(w_out.shape),
            ],
            out_specs=tile_spec,
            scratch_shapes=[pltpu.VMEM((side + 2, side + 2 * OFF, channels), jnp.float32)],
        ),
        name="block",
    )(pick, flat_flip, cells, cand, dw_weight, vec, w_in, b_in.reshape(1, hidden), w_out)


def solution(mesh):
    spread_spec = P(AXES, None, None, None)
    in_specs = (spread_spec, P(AXES, None), P(AXES, None)) + (P(),) * 9
    return jax.shard_map(
        per_device, mesh=mesh, in_specs=in_specs, out_specs=spread_spec, check_vma=False
    )
```

time: 87.7 us -> 48.4 us (0.55)
  matrix products: 47.4 us -> 0 us
  Pallas kernels: 0 us -> 29.9 us
  other arithmetic: 27.8 us -> 1.46 us
  waiting for transfers between devices: 0.01 us -> 3.51 us
  local copies, waits for them, and re-layouts: 5.33 us -> 6.77 us
    dot_general x2 -> x0, matrix products: 47.4 us -> none  [the longest x1 44.8 us: per_device(): lax.dot_general(normed, w_in, (((1,), (1,)), ((), ())), preferred_element...]
    pallas_call x0 -> x1, Pallas kernels: none -> 29.9 us  [per_device(): pl.pallas_call(functools.partial(block_kernel, 4), out_shape=jax.ShapeDty...]
    convert_element_type x5 -> x0, other arithmetic: 11.2 us -> none  [the longest x1 4.19 us: per_device(): cells.astype(jnp.float32) + layer_scale * mixed]
    reduce_sum x2 -> x0, other arithmetic: 9.8 us -> none  [the longest x1 7.03 us: layer_norm(): center = jnp.mean(conv, axis=-1, keepdims=True)]
    concatenate x2 -> x1, other arithmetic: 5.04 us -> 0.89 us  [per_device(): cand = jnp.concatenate([before, rims, after], axis=0)]
    ppermute x2, waiting for transfers between devices: 0.01 us -> 3.51 us  [shifted(): lax.ppermute(array, AXES, [(i, (i + by) % count) for i in range(count)])]
    reshape x0 -> x2, local copies, waits for them, and re-layouts: none -> 2.55 us  [the longest x1 1.31 us: per_device(): flat_flip = edge_flip.reshape(edge_count)]
    mul x1 -> x0, local copies, waits for them, and re-layouts: 1.59 us -> none  [depthwise(): dw_weight[3 * row_tap + col_tap]]
  transfers between devices with their start and end apart: 2 -> 2, of which waited for: 0 -> 1; matrix products, arithmetic and copies ran while one was open for 10% -> 11% of each run, Pallas kernels for 0% -> 0%
where the time goes in v1:
time: 48.4 us; the launch traced here: 48.1 us
  Pallas kernels  29.9 us (62%)
  local copies, waits for them, and re-layouts  6.77 us (14%)
  starting transfers between devices  6.46 us (13%)
  waiting for transfers between devices  3.51 us (7%)
  other arithmetic  1.46 us (3%)
    pallas_call x1, Pallas kernels, per_device(): pl.pallas_call(functools.partial(block_kernel, 4), out_shape=jax.ShapeDty...  29.9 us
    ppermute x2, starting transfers between devices, shifted(): lax.ppermute(array, AXES, [(i, (i + by) % count) for i in range(count)])  6.46 us
    ppermute x2, waiting for transfers between devices, shifted(): lax.ppermute(array, AXES, [(i, (i + by) % count) for i in range(count)])  3.51 us
    another operation x1, local copies, waits for them, and re-layouts, per_device(): vec = jnp.stack([dw_bias, ln_gain, ln_bias, b_out, layer_scale], axis=0)  1.32 us
    reshape x1, local copies, waits for them, and re-layouts, per_device(): flat_flip = edge_flip.reshape(edge_count)  1.31 us
    slice x1, local copies, waits for them, and re-layouts, boundary(): tiles_in[:, :, -1]  1.28 us
    reshape x1, local copies, waits for them, and re-layouts, per_device(): b_in.reshape(1, hidden)  1.25 us
  transfers between devices with their start and end apart: 2, of which 1 were waited for; matrix products, arithmetic and copies ran while one was open for 11% of the time, Pallas kernels for 0%

profile of v1, /device:TPU:0, one launch (start us, length us, event | category | flops | bytes accessed | tf_op | source)
XLA Modules:
  0.0 48.1 jit_solution(8582070201805887789)
XLA Ops:
  0.0 0.8 %fusion.3 = (bf16[4,1,48,128]{3,2,1,0:T(8,128)(2,1)S(1)}, bf16[4,1,48,128]{3,2,1,0:T(8,128)(2,1)S(1)}) fusion(bf16[4,48,48,128]{3,2,1,0:T(8,128)(2,1)} %cells_ref.1), kind=kLoop, calls=%fused_computation.17 | loop fusion | bytes 196608 | tf_op jit(solution)/shard_map/slice | solution.py:21
  0.8 1.3 %fusion.4 = (bf16[4,48,1,128]{3,2,1,0:T(2,128)(2,1)S(1)}, bf16[4,48,1,128]{3,2,1,0:T(2,128)(2,1)S(1)}) fusion(bf16[4,48,48,128]{3,2,1,0:T(8,128)(2,1)} %cells_ref.1), kind=kLoop, calls=%fused_computation.18 | loop fusion | bytes 196608 | tf_op jit(solution)/shard_map/slice | solution.py:21
  2.2 6.5 %collective-permute-start.1 = (bf16[16,48,128]{2,1,0:T(8,128)(2,1)S(1)}, bf16[16,48,128]{2,1,0:T(8,128)(2,1)S(1)}, u32[]{:S(2)}, u32[]{:S(2)}) collective-permute-start(bf16[16,48,128]{2,1,0:T(8,128)(2,1)S(1)} %bitcast.10), channel_id=1, source_target_pairs={{0,31},{1,0},{2,1},{3,2},{4,3},{5,4},{6,5},{7,6},{8,7},{9,8},{10,9... | collective-permute-start | bytes 589832 | tf_op jit(solution)/shard_map/ppermute | solution.py:16
  8.6 0.0 collective-permute-start
  8.6 0.8 %reshape.12 = s32[16]{0:T(128)S(1)} reshape(s32[4,4]{1,0:T(4,128)} %param.13) | data formatting | bytes 128 | tf_op jit(solution)/shard_map/reshape | solution.py:125
  9.4 1.3 %reshape.13.flip_ref = s32[16]{0:T(128)} reshape(s32[4,4]{1,0:T(4,128)} %param.14) | data formatting | bytes 128 | tf_op jit(solution)/shard_map/reshape | solution.py:126
  10.7 1.2 %reshape.15.b_in_ref = bf16[1,512]{1,0:T(2,128)(2,1)} reshape(bf16[512]{0:T(512)(128)(2,1)} %param.20) | data formatting | bytes 2048 | tf_op jit(solution)/shard_map/reshape | solution.py:159
  12.0 1.3 %stack.27.vec_ref = f32[5,128]{1,0:T(8,128)} concatenate(f32[1,128]{1,0:T(1,128)} %bitcast.13, f32[1,128]{1,0:T(1,128)} %bitcast.14, f32[1,128]{1,0:T(1,128)} %bitcast.15, f32[1,128]{1,0:T(1,128)} %bitcast.16, f32[1,128]{1,0:T(1,128)} %bitcast.17), dimensions={0} | concatenate | bytes 5120 | tf_op jit(solution)/shard_map/stack | solution.py:134
  13.3 0.5 %fusion.pick_ref = s32[16]{0:T(128)} fusion(s32[16]{0:T(128)S(1)} %reshape.12, s32[]{:T(128)S(6)} %add.17), kind=kLoop, calls=%fused_computation.14 | loop fusion | flops 592 | bytes 132 | tf_op jit(solution)/shard_map/add | solution.py:130
  13.8 0.0 collective-permute-done.1
  13.8 3.5 %collective-permute-done = bf16[16,48,128]{2,1,0:T(8,128)(2,1)S(1)} collective-permute-done((bf16[16,48,128]{2,1,0:T(8,128)(2,1)S(1)}, bf16[16,48,128]{2,1,0:T(8,128)(2,1)S(1)}, u32[]{:S(2)}, u32[]{:S(2)}) %collective-permute-start) | collective-permute-done | bytes 196640 | tf_op jit(solution)/shard_map/ppermute | solution.py:16
  17.3 0.9 %pad_maximum_fusion.cand_ref = bf16[48,48,128]{2,1,0:T(8,128)(2,1)} fusion(bf16[16,48,128]{2,1,0:T(8,128)(2,1)S(1)} %collective-permute-done.1, bf16[16,48,128]{2,1,0:T(8,128)(2,1)S(1)} %bitcast.12, bf16[16,48,128]{2,1,0:T(8,128)(2,1)S(1)} %collective-permute-done), kind=kLoop, calls=%fused_computation | loop fusion | flops 589824 | bytes 1179648 | tf_op jit(solution)/shard_map/concatenate | solution.py:133
  18.2 29.9 %block.1 = bf16[4,48,48,128]{3,2,1,0:T(8,128)(2,1)} custom-call(s32[16]{0:T(128)} %fusion.pick_ref, s32[16]{0:T(128)} %reshape.13.flip_ref, bf16[4,48,48,128]{3,2,1,0:T(8,128)(2,1)} %cells_ref.1, bf16[48,48,128]{2,1,0:T(8,128)(2,1)} %pad_maximum_fusion.cand_ref, f32[9,128]{1,0:T(8,128)} %dw_ref.1, f32[5,128]{1,0:T(8,128)} %stack.27.vec_ref, ...), custom_call_target="tpu_custom_call" | custom-call | tf_op jit(solution)/shard_map/block/pallas_call | solution.py:140
  (2 shorter events, 0.0 us)
Async XLA Ops:
  2.2 11.6 %collective-permute-start.1 = (bf16[16,48,128]{2,1,0:T(8,128)(2,1)S(1)}, bf16[16,48,128]{2,1,0:T(8,128)(2,1)S(1)}, u32[]{:S(2)}, u32[]{:S(2)}) collective-permute-start(bf16[16,48,128]{2,1,0:T(8,128)(2,1)S(1)} %bitcast.10), channel_id=1, source_target_pairs={{0,31},{1,0},{2,1},{3,2},{4,3},{5,4},{6,5},{7,6},{8,7},{9,8},{10,9... | collective-permute-start | bytes 589832 | tf_op jit(solution)/shard_map/ppermute | solution.py:16
  8.6 8.7 %collective-permute-start = (bf16[16,48,128]{2,1,0:T(8,128)(2,1)S(1)}, bf16[16,48,128]{2,1,0:T(8,128)(2,1)S(1)}, u32[]{:S(2)}, u32[]{:S(2)}) collective-permute-start(bf16[16,48,128]{2,1,0:T(8,128)(2,1)S(1)} %bitcast.11), channel_id=1, source_target_pairs={{0,1},{1,2},{2,3},{3,4},{4,5},{5,6},{6,7},{7,8},{8,9},{9,10},{10,1... | collective-permute-start | bytes 589832 | tf_op jit(solution)/shard_map/ppermute | solution.py:16

commit v2 on v1

v2 whole, which is shorter than its diff:
```python
import functools

import jax
import jax.numpy as jnp
from jax import lax
from jax.experimental import pallas as pl
from jax.experimental.pallas import tpu as pltpu
from jax.sharding import PartitionSpec as P

AXES = ("tile", "hidden")
OFF = 8
CELLS_PER_CHUNK = 256
MESH = pl.DeviceIdType.MESH
ROOT_HALF = 0.7071067811865476


def divisor(total, limit):
    return max(d for d in range(1, min(total, limit) + 1) if total % d == 0)


def block_kernel(
    sizes,
    partner_ref,
    flip_ref,
    cells_ref,
    dw_ref,
    dw_bias_ref,
    gain_ref,
    bias_ref,
    w_in_ref,
    b_in_ref,
    w_out_ref,
    b_out_ref,
    scale_ref,
    out_ref,
    cells_buf,
    pad_ref,
    cand_ref,
    w_aug_ref,
    buf_a,
    buf_b,
    load_sem,
    send_sem,
    recv_sem,
):
    tile_devices, hidden_devices = sizes
    tiles, side, _, channels = out_ref.shape
    edges = 4 * tiles
    width = side + 2 * OFF
    devices = tile_devices * hidden_devices
    me = lax.axis_index("tile") * hidden_devices + lax.axis_index("hidden")

    def at(position):
        return (position // hidden_devices, position % hidden_devices)

    right = lax.rem(me + 1, devices)
    left = lax.rem(me + devices - 1, devices)

    loads = [
        pltpu.make_async_copy(cells_ref.at[t], cells_buf.at[t], load_sem.at[t])
        for t in range(tiles)
    ]
    for copy in loads:
        copy.start()
    barrier = pltpu.get_barrier_semaphore()
    for neighbour in (left, right):
        pl.semaphore_signal(barrier, inc=1, device_id=at(neighbour), device_id_type=MESH)

    hidden = w_in_ref.shape[0]
    eye = (
        lax.broadcasted_iota(jnp.int32, (channels, channels), 0)
        == lax.broadcasted_iota(jnp.int32, (channels, channels), 1)
    ).astype(jnp.bfloat16)
    w_aug_ref[0:channels, :] = lax.dot_general(
        eye, w_in_ref[...], (((1,), (1,)), ((), ())), preferred_element_type=jnp.float32
    ).astype(jnp.bfloat16)
    b_in = b_in_ref[...].astype(jnp.float32).reshape(1, hidden) * ROOT_HALF
    b_high = b_in.astype(jnp.bfloat16).astype(jnp.float32)
    row_id = lax.broadcasted_iota(jnp.int32, (channels, hidden), 0)
    extra = jnp.where(row_id == 0, b_high, jnp.where(row_id == 1, b_in - b_high, 0.0))
    w_aug_ref[channels : 2 * channels, :] = extra.astype(jnp.bfloat16)
    lane_id = lax.broadcasted_iota(jnp.int32, (buf_a.shape[0], channels), 1)
    ones = jnp.where(lane_id < 2, 1.0, 0.0).astype(jnp.bfloat16)
    buf_a[:, channels : 2 * channels] = ones
    buf_b[:, channels : 2 * channels] = ones

    flat_pad = pad_ref.reshape(tiles * (side + 2) * width, channels)
    for t in range(tiles):
        loads[t].wait()
        top = t * (side + 2)
        pad_ref[pl.ds(top + 1, side), pl.ds(OFF, side), :] = cells_buf[t].astype(jnp.float32)
        first = (top + 1) * width + OFF
        cand_ref[edges + 4 * t] = cells_buf[t, 0]
        cand_ref[edges + 4 * t + 2] = cells_buf[t, side - 1]
        east = flat_pad[pl.ds(first + side - 1, side, stride=width), :]
        cand_ref[edges + 4 * t + 1] = east.astype(jnp.bfloat16)
        west = flat_pad[pl.ds(first, side, stride=width), :]
        cand_ref[edges + 4 * t + 3] = west.astype(jnp.bfloat16)

    pl.semaphore_wait(barrier, 2)
    own = cand_ref.at[pl.ds(edges, edges)]
    sends = [
        pltpu.make_async_remote_copy(
            src_ref=own,
            dst_ref=cand_ref.at[pl.ds(slot * edges, edges)],
            send_sem=send_sem.at[slot // 2],
            recv_sem=recv_sem.at[slot // 2],
            device_id=at(target),
            device_id_type=MESH,
        )
        for slot, target in ((0, right), (2, left))
    ]
    for copy in sends:
        copy.start()

    dw_bias = dw_bias_ref[...]
    gain = gain_ref[...] * ROOT_HALF
    bias = bias_ref[...] * ROOT_HALF
    out_scale = scale_ref[...] * ROOT_HALF
    out_bias = scale_ref[...] * b_out_ref[...]
    taps = [dw_ref[k : k + 1] for k in range(9)]

    def conv(segments, dst):
        place = 0
        for tile, row, col, count in segments:
            line = tile * (side + 2) + row
            total = jnp.broadcast_to(dw_bias, (count, channels))
            for a in range(3):
                for b in range(3):
                    total = total + taps[3 * a + b] * pad_ref[
                        line + a, pl.ds(OFF - 1 + b + col, count), :
                    ]
            center = total - jnp.mean(total, axis=-1, keepdims=True)
            spread = jnp.mean(center * center, axis=-1, keepdims=True)
            value = center * lax.rsqrt(spread + 1e-06) * gain + bias
            dst[place : place + count, 0:channels] = value.astype(jnp.bfloat16)
            place += count

    def mlp(segments, src):
        z = jnp.dot(src[...], w_aug_ref[...], preferred_element_type=jnp.float32)
        act = (z + z * lax.erf(z)).astype(jnp.bfloat16)
        mixed = jnp.dot(act, w_out_ref[...], preferred_element_type=jnp.float32)
        mixed = mixed * out_scale + out_bias
        place = 0
        for tile, row, col, count in segments:
            line = tile * (side + 2) + row + 1
            old = pad_ref[line, pl.ds(OFF + col, count), :]
            new = old + mixed[place : place + count]
            out_ref[tile, row, pl.ds(col, count), :] = new.astype(out_ref.dtype)
            place += count

    inner_cols = side - 2 * OFF
    inner_rows = side - 2
    rows_in = CELLS_PER_CHUNK // inner_cols
    rows_edge = CELLS_PER_CHUNK // (2 * OFF)

    def inner(chunk):
        found = []
        for k in range(rows_in):
            q = chunk * rows_in + k
            found.append((q // inner_rows, q % inner_rows + 1, OFF, inner_cols))
        return found

    def caps():
        return [(t, r, OFF, inner_cols) for t in range(tiles) for r in (0, side - 1)]

    def sides(chunk):
        found = []
        per_tile = side // rows_edge
        for k in range(rows_edge):
            tile = chunk // per_tile
            row = (chunk % per_tile) * rows_edge + k
            found += [(tile, row, 0, OFF), (tile, row, side - OFF, OFF)]
        return found

    inner_chunks = tiles * inner_rows // rows_in
    side_chunks = tiles * side // rows_edge

    conv(inner(0), buf_a)

    @pl.loop(0, inner_chunks // 2)
    def _(i):
        mlp(inner(2 * i), buf_a)
        conv(inner(2 * i + 1), buf_b)
        mlp(inner(2 * i + 1), buf_b)
        conv(inner(2 * i + 2), buf_a)

    for copy in sends:
        copy.wait()
    r_id = lax.broadcasted_iota(jnp.int32, (side, side), 0)
    c_id = lax.broadcasted_iota(jnp.int32, (side, side), 1)
    for t in range(tiles):
        lines = []
        for s in range(4):
            partner = partner_ref[t, s]
            distance = lax.rem(partner // edges - me + devices, devices)
            group = jnp.where(distance == devices - 1, 0, jnp.where(distance == 1, 2, 1))
            target = jnp.where(flip_ref[t, s] == 1, side - 1 - r_id, r_id)
            order = jnp.where(c_id == target, 1.0, 0.0).astype(jnp.bfloat16)
            line = cand_ref[group * edges + lax.rem(partner, edges)]
            lines.append(jnp.dot(order, line, preferred_element_type=jnp.float32))
        north, east, south, west = lines
        top = t * (side + 2)
        end = top + side + 1
        pad_ref[top, pl.ds(OFF, side), :] = north
        pad_ref[end, pl.ds(OFF, side), :] = south
        first = (top + 1) * width + OFF
        flat_pad[pl.ds(first - 1, side, stride=width), :] = west
        flat_pad[pl.ds(first + side, side, stride=width), :] = east
        pad_ref[top, OFF - 1 : OFF, :] = 0.5 * (north[:1] + west[:1])
        pad_ref[top, OFF + side : OFF + side + 1, :] = 0.5 * (north[-1:] + east[:1])
        pad_ref[end, OFF - 1 : OFF, :] = 0.5 * (south[:1] + west[-1:])
        pad_ref[end, OFF + side : OFF + side + 1, :] = 0.5 * (south[-1:] + east[-1:])

    mlp(inner(inner_chunks - 1), buf_a)
    conv(caps(), buf_b)
    mlp(caps(), buf_b)
    conv(sides(0), buf_a)

    @pl.loop(0, side_chunks // 2 - 1)
    def _(i):
        mlp(sides(2 * i), buf_a)
        conv(sides(2 * i + 1), buf_b)
        mlp(sides(2 * i + 1), buf_b)
        conv(sides(2 * i + 2), buf_a)

    mlp(sides(side_chunks - 2), buf_a)
    conv(sides(side_chunks - 1), buf_b)
    mlp(sides(side_chunks - 1), buf_b)


def per_device(
    sizes,
    cells,
    partner_edge,
    edge_flip,
    dw_weight,
    dw_bias,
    ln_gain,
    ln_bias,
    w_in,
    b_in,
    w_out,
    b_out,
    layer_scale,
):
    tiles, side, _, channels = cells.shape
    hidden = w_in.shape[0]
    edges = 4 * tiles
    vmem = pl.BlockSpec(memory_space=pltpu.VMEM)
    smem = pl.BlockSpec(memory_space=pltpu.SMEM)

    def row(vector):
        return vector.reshape(1, channels)

    return pl.pallas_call(
        functools.partial(block_kernel, sizes),
        out_shape=jax.ShapeDtypeStruct(cells.shape, jnp.bfloat16),
        in_specs=[smem, smem, pl.BlockSpec(memory_space=pl.ANY)] + [vmem] * 9,
        out_specs=vmem,
        scratch_shapes=[
            pltpu.VMEM(cells.shape, jnp.bfloat16),
            pltpu.VMEM((tiles * (side + 2), side + 2 * OFF, channels), jnp.float32),
            pltpu.VMEM((3 * edges, side, channels), jnp.bfloat16),
            pltpu.VMEM((2 * channels, hidden), jnp.bfloat16),
            pltpu.VMEM((CELLS_PER_CHUNK, 2 * channels), jnp.bfloat16),
            pltpu.VMEM((CELLS_PER_CHUNK, 2 * channels), jnp.bfloat16),
            pltpu.SemaphoreType.DMA((tiles,)),
            pltpu.SemaphoreType.DMA((2,)),
            pltpu.SemaphoreType.DMA((2,)),
        ],
        compiler_params=pltpu.CompilerParams(collective_id=0, has_side_effects=True),
        name="block",
    )(
        partner_edge,
        edge_flip,
        cells,
        dw_weight,
        row(dw_bias),
        row(ln_gain),
        row(ln_bias),
        w_in,
        b_in,
        w_out,
        row(b_out),
        row(layer_scale),
    )


def solution(mesh):
    spread_spec = P(AXES, None, None, None)
    in_specs = (spread_spec, P(AXES, None), P(AXES, None)) + (P(),) * 9
    sizes = (mesh.shape["tile"], mesh.shape["hidden"])
    return jax.shard_map(
        functools.partial(per_device, sizes),
        mesh=mesh,
        in_specs=in_specs,
        out_specs=spread_spec,
        check_vma=False,
    )
```

time: 48.4 us -> 25 us (0.52)
  Pallas kernels: 29.9 us -> 21.4 us
  starting transfers between devices: 6.46 us -> 0 us
  waiting for transfers between devices: 3.51 us -> 0 us
  local copies, waits for them, and re-layouts: 6.77 us -> 3.48 us
  other arithmetic: 1.46 us -> 0 us
    pallas_call x1, Pallas kernels: 29.9 us -> 21.4 us  [per_device(): pl.pallas_call(functools.partial(block_kernel, sizes), out_shape=jax.Shap...]
    ppermute x2 -> x0, starting transfers between devices: 6.46 us -> none  [shifted(): lax.ppermute(array, AXES, [(i, (i + by) % count) for i in range(count)])]
    ppermute x2 -> x0, waiting for transfers between devices: 3.51 us -> none  [shifted(): lax.ppermute(array, AXES, [(i, (i + by) % count) for i in range(count)])]
    unnamed x0 -> x1, local copies, waits for them, and re-layouts: none -> 3.48 us
    reshape x3 -> x0, local copies, waits for them, and re-layouts: 3.32 us -> none  [the longest x1 1.31 us: per_device(): flat_flip = edge_flip.reshape(edge_count)]
    slice x2 -> x0, local copies, waits for them, and re-layouts: 2.11 us -> none  [the longest x1 1.28 us: boundary(): tiles_in[:, :, -1]]
    another operation x2 -> x0, local copies, waits for them, and re-layouts: 1.34 us -> none  [the longest x1 1.32 us: per_device(): vec = jnp.stack([dw_bias, ln_gain, ln_bias, b_out, layer_scale], axis=0)]
    concatenate x1 -> x0, other arithmetic: 0.89 us -> none  [per_device(): cand = jnp.concatenate([before, rims, after], axis=0)]
  transfers between devices with their start and end apart: 2 -> 0, of which waited for: 1 -> 0; matrix products, arithmetic and copies ran while one was open for 11% -> 0% of each run, Pallas kernels for 0% -> 0%
where the time goes in v2:
time: 25 us; the launch traced here: 24.8 us
  Pallas kernels  21.4 us (86%)
  local copies, waits for them, and re-layouts  3.48 us (14%)
    pallas_call x1, Pallas kernels, per_device(): pl.pallas_call(functools.partial(block_kernel, sizes), out_shape=jax.Shap...  21.4 us
    unnamed x1, local copies, waits for them, and re-layouts  3.48 us

profile of v2, /device:TPU:0, one launch (start us, length us, event | category | flops | bytes accessed | tf_op | source)
XLA Modules:
  0.0 24.8 jit_solution(10899409616076222583)
XLA Ops:
  0.0 21.4 %block.1 = bf16[4,48,48,128]{3,2,1,0:T(8,128)(2,1)} custom-call(s32[4,4]{1,0:T(4,128)} %partner_ref.1, s32[4,4]{1,0:T(4,128)} %flip_ref.1, bf16[4,48,48,128]{3,2,1,0:T(8,128)(2,1)} %cells_ref.1, f32[9,128]{1,0:T(8,128)} %dw_ref.1, f32[1,128]{1,0:T(1,128)} %bitcast.5, f32[1,128]{1,0:T(1,128)} %bitcast.6, f32[1,128]{1,0:T(1,128)} %bitcast.7, ...), custom_call_target="tpu_custom_call" | custom-call | tf_op jit(solution)/shard_map/block/pallas_call | solution.py:256
  21.4 3.5 %copy.14 = bf16[4,48,48,128]{3,2,1,0:T(8,128)(2,1)} copy(bf16[4,48,48,128]{3,2,1,0:T(8,128)(2,1)} %block.1) | data formatting | bytes 4718592

commit v3 on v2

v3 whole, which is shorter than its diff:
```python
import functools

import jax
import jax.numpy as jnp
from jax import lax
from jax.experimental import pallas as pl
from jax.experimental.pallas import tpu as pltpu
from jax.sharding import PartitionSpec as P

AXES = ("tile", "hidden")
OFF = 8
CELLS_PER_CHUNK = 256
UNROLL = 4
CROSS = 4
GRANT = 32 * 1024 * 1024
MESH = pl.DeviceIdType.MESH
ROOT_HALF = 0.7071067811865476


def tile_of(q, per_tile, tiles):
    tile = 0
    for j in range(1, tiles):
        tile = tile + jnp.where(q >= j * per_tile, 1, 0)
    return tile


def conv(taps, vectors, pad_ref, side, segments, dst):
    dw_bias, gain, bias = vectors
    channels = pad_ref.shape[2]
    start = 0
    for tile, row, col, count in segments:
        line = tile * (side + 2) + row
        total = jnp.broadcast_to(dw_bias, (count, channels))
        for a in range(3):
            for b in range(3):
                total = total + taps[3 * a + b] * pad_ref[
                    line + a, pl.ds(OFF - 1 + b + col, count), :
                ]
        center = total - jnp.mean(total, axis=-1, keepdims=True)
        spread = jnp.sum(center * center, axis=-1, keepdims=True)
        value = center * lax.rsqrt(spread + 1e-06 * channels) * gain + bias
        dst[start : start + count, 0:channels] = value.astype(jnp.bfloat16)
        start += count


def mlp(w_aug_ref, w_out_ref, vectors, pad_ref, out_ref, segments, src):
    out_scale, out_bias = vectors
    side = out_ref.shape[1]
    z = jnp.dot(src[...], w_aug_ref[...], preferred_element_type=jnp.float32)
    act = (z + z * lax.erf(z)).astype(jnp.bfloat16)
    mixed = jnp.dot(act, w_out_ref[...], preferred_element_type=jnp.float32)
    mixed = mixed * out_scale + out_bias
    start = 0
    for tile, row, col, count in segments:
        line = tile * (side + 2) + row + 1
        old = pad_ref[line, pl.ds(OFF + col, count), :]
        new = old + mixed[start : start + count]
        out_ref[tile, row, pl.ds(col, count), :] = new.astype(out_ref.dtype)
        start += count


def vectors_of(dw_ref, dw_bias_ref, gain_ref, bias_ref, b_out_ref, scale_ref):
    channels = dw_ref.shape[1]
    taps = [dw_ref[k : k + 1] for k in range(9)]
    gain = gain_ref[...] * (ROOT_HALF * channels**0.5)
    first = (dw_bias_ref[...], gain, bias_ref[...] * ROOT_HALF)
    last = (scale_ref[...] * ROOT_HALF, scale_ref[...] * b_out_ref[...])
    return taps, first, last


def fill_ones(buf):
    rows, both = buf.shape
    lane = lax.broadcasted_iota(jnp.int32, (rows, both // 2), 1)
    buf[:, both // 2 :] = jnp.where(lane < 2, 1.0, 0.0).astype(jnp.bfloat16)


def last_flagged(flags, values):
    found = [jnp.int32(0)] * CROSS
    for flag, value in zip(flags, values):
        for k in range(CROSS - 1, 0, -1):
            found[k] = jnp.where(flag, found[k - 1], found[k])
        found[0] = jnp.where(flag, value, found[0])
    return found


def owned(partner, device, edges):
    local = partner - device * edges
    return (local >= 0) & (local < edges), local


def inner_kernel(
    sizes,
    partner_ref,
    cells_ref,
    dw_ref,
    dw_bias_ref,
    gain_ref,
    bias_ref,
    w_in_ref,
    b_in_ref,
    w_out_ref,
    b_out_ref,
    scale_ref,
    out_ref,
    pad_ref,
    rims_ref,
    recv_ref,
    w_aug_ref,
    cells_buf,
    send_buf,
    buf_a,
    buf_b,
    load_sem,
    send_sem,
    recv_sem,
):
    tile_devices, hidden_devices = sizes
    tiles, side, _, channels = out_ref.shape
    edges = 4 * tiles
    width = side + 2 * OFF
    devices = tile_devices * hidden_devices
    me = lax.axis_index("tile") * hidden_devices + lax.axis_index("hidden")

    def at(position):
        return (position // hidden_devices, position % hidden_devices)

    right = lax.rem(me + 1, devices)
    left = lax.rem(me + devices - 1, devices)
    loads = [
        pltpu.make_async_copy(cells_ref.at[t], cells_buf.at[t], load_sem.at[t])
        for t in range(tiles)
    ]
    for copy in loads:
        copy.start()
    barrier = pltpu.get_barrier_semaphore()
    for neighbour in (left, right):
        pl.semaphore_signal(barrier, inc=1, device_id=at(neighbour), device_id_type=MESH)

    partners = [partner_ref[e // 4, e % 4] for e in range(edges)]
    local = [jnp.int32(e) for e in range(edges)]
    going = []
    for device in (right, left):
        going += last_flagged([owned(p, device, edges)[0] for p in partners], local)

    flat_pad = pad_ref.reshape(tiles * (side + 2) * width, channels)
    for t in range(tiles):
        loads[t].wait()
        top = t * (side + 2)
        pad_ref[pl.ds(top + 1, side), pl.ds(OFF, side), :] = cells_buf[t].astype(jnp.float32)
        first = (top + 1) * width + OFF
        mine = 4 * t
        rims_ref[mine] = cells_buf[t, 0]
        rims_ref[mine + 2] = cells_buf[t, side - 1]
        east = flat_pad[pl.ds(first + side - 1, side, stride=width), :]
        rims_ref[mine + 1] = east.astype(jnp.bfloat16)
        west = flat_pad[pl.ds(first, side, stride=width), :]
        rims_ref[mine + 3] = west.astype(jnp.bfloat16)
    for k in range(2 * CROSS):
        send_buf[k] = rims_ref[going[k]]

    pl.semaphore_wait(barrier, 2)
    sends = [
        pltpu.make_async_remote_copy(
            src_ref=send_buf.at[pl.ds(side_id * CROSS, CROSS)],
            dst_ref=recv_ref.at[pl.ds(side_id * CROSS, CROSS)],
            send_sem=send_sem.at[side_id],
            recv_sem=recv_sem.at[side_id],
            device_id=at(target),
            device_id_type=MESH,
        )
        for side_id, target in ((0, right), (1, left))
    ]
    for copy in sends:
        copy.start()

    hidden = w_in_ref.shape[0]
    eye = (
        lax.broadcasted_iota(jnp.int32, (channels, channels), 0)
        == lax.broadcasted_iota(jnp.int32, (channels, channels), 1)
    ).astype(jnp.bfloat16)
    w_aug_ref[0:channels, :] = lax.dot_general(
        eye, w_in_ref[...], (((1,), (1,)), ((), ())), preferred_element_type=jnp.float32
    ).astype(jnp.bfloat16)
    b_in = b_in_ref[...].astype(jnp.float32).reshape(1, hidden) * ROOT_HALF
    b_high = b_in.astype(jnp.bfloat16).astype(jnp.float32)
    row_id = lax.broadcasted_iota(jnp.int32, (channels, hidden), 0)
    extra = jnp.where(row_id == 0, b_high, jnp.where(row_id == 1, b_in - b_high, 0.0))
    w_aug_ref[channels : 2 * channels, :] = extra.astype(jnp.bfloat16)
    fill_ones(buf_a)
    fill_ones(buf_b)

    taps, first, last = vectors_of(
        dw_ref, dw_bias_ref, gain_ref, bias_ref, b_out_ref, scale_ref
    )
    do_conv = functools.partial(conv, taps, first, pad_ref, side)
    do_mlp = functools.partial(mlp, w_aug_ref, w_out_ref, last, pad_ref, out_ref)
    inner_cols = side - 2 * OFF
    inner_rows = side - 2
    rows_in = CELLS_PER_CHUNK // inner_cols

    def inner(chunk):
        found = []
        for k in range(rows_in):
            q = chunk * rows_in + k
            tile = tile_of(q, inner_rows, tiles)
            found.append((tile, q - inner_rows * tile + 1, OFF, inner_cols))
        return found

    chunks = tiles * inner_rows // rows_in
    bufs = (buf_a, buf_b)
    do_conv(inner(0), buf_a)

    @pl.loop(0, (chunks - 1) // UNROLL)
    def _(i):
        for u in range(UNROLL):
            do_mlp(inner(UNROLL * i + u), bufs[u % 2])
            do_conv(inner(UNROLL * i + u + 1), bufs[(u + 1) % 2])

    for c in range((chunks - 1) // UNROLL * UNROLL, chunks):
        do_mlp(inner(c), bufs[c % 2])
        if c + 1 < chunks:
            do_conv(inner(c + 1), bufs[(c + 1) % 2])
    for copy in sends:
        copy.wait()


def edge_kernel(
    sizes,
    partner_ref,
    flip_ref,
    inner_ref,
    pad_in_ref,
    rims_ref,
    recv_ref,
    w_aug_ref,
    dw_ref,
    dw_bias_ref,
    gain_ref,
    bias_ref,
    w_out_ref,
    b_out_ref,
    scale_ref,
    out_hbm,
    pad_ref,
    out_ref,
    buf_a,
    buf_b,
    inner_sem,
    store_sem,
):
    tile_devices, hidden_devices = sizes
    tiles, side, _, channels = out_ref.shape
    edges = 4 * tiles
    width = side + 2 * OFF
    devices = tile_devices * hidden_devices
    inner_cols = side - 2 * OFF
    me = lax.axis_index("tile") * hidden_devices + lax.axis_index("hidden")
    right = lax.rem(me + 1, devices)
    left = lax.rem(me + devices - 1, devices)

    def piece(t, rows, first_row, cols, first_col):
        return (t, pl.ds(first_row, rows), pl.ds(first_col, cols))

    inner_copies = []
    for t in range(tiles):
        part = piece(t, side - 2, 1, inner_cols, OFF)
        inner_copies.append(
            pltpu.make_async_copy(inner_ref.at[part], out_hbm.at[part], inner_sem.at[t])
        )
    for copy in inner_copies:
        copy.start()

    partners = [partner_ref[e // 4, e % 4] for e in range(edges)]
    prev_flags, prev_local = zip(*[owned(p, left, edges) for p in partners])
    next_flags, next_local = zip(*[owned(p, right, edges) for p in partners])
    prev_list = last_flagged(prev_flags, prev_local)
    next_list = last_flagged(next_flags, next_local)

    def above(values, limit):
        return sum(jnp.where(value > limit, 1, 0) for value in values)

    flat_pad = pad_ref.reshape(tiles * (side + 2) * width, channels)
    r_id = lax.broadcasted_iota(jnp.int32, (side, side), 0)
    c_id = lax.broadcasted_iota(jnp.int32, (side, side), 1)
    for t in range(tiles):
        lines = []
        for s in range(4):
            e = 4 * t + s
            is_prev, is_next = prev_flags[e], next_flags[e]
            slot = jnp.where(
                is_prev,
                above(prev_list, prev_local[e]),
                CROSS + above(next_list, next_local[e]),
            )
            crosses = is_prev | is_next
            own_edge = jnp.where(crosses, 0, partners[e] - me * edges)
            received = recv_ref[jnp.where(crosses, slot, 0)]
            line = jnp.where(crosses, received, rims_ref[own_edge])
            target = jnp.where(flip_ref[t, s] == 1, side - 1 - r_id, r_id)
            order = jnp.where(c_id == target, 1.0, 0.0).astype(jnp.bfloat16)
            lines.append(jnp.dot(order, line, preferred_element_type=jnp.float32))
        north, east, south, west = lines
        top = t * (side + 2)
        end = top + side + 1
        pad_ref[top, pl.ds(OFF, side), :] = north
        pad_ref[end, pl.ds(OFF, side), :] = south
        first = (top + 1) * width + OFF
        flat_pad[pl.ds(first - 1, side, stride=width), :] = west
        flat_pad[pl.ds(first + side, side, stride=width), :] = east
        pad_ref[top, OFF - 1 : OFF, :] = 0.5 * (north[:1] + west[:1])
        pad_ref[top, OFF + side : OFF + side + 1, :] = 0.5 * (north[-1:] + east[:1])
        pad_ref[end, OFF - 1 : OFF, :] = 0.5 * (south[:1] + west[-1:])
        pad_ref[end, OFF + side : OFF + side + 1, :] = 0.5 * (south[-1:] + east[-1:])

    fill_ones(buf_a)
    fill_ones(buf_b)
    taps, first, last = vectors_of(
        dw_ref, dw_bias_ref, gain_ref, bias_ref, b_out_ref, scale_ref
    )
    do_conv = functools.partial(conv, taps, first, pad_ref, side)
    do_mlp = functools.partial(mlp, w_aug_ref, w_out_ref, last, pad_ref, out_ref)
    caps = [(t, r, OFF, inner_cols) for t in range(tiles) for r in (0, side - 1)]
    rows_edge = CELLS_PER_CHUNK // (2 * OFF)
    per_tile = side // rows_edge

    def sides(chunk):
        found = []
        for k in range(rows_edge):
            tile = chunk // per_tile
            row = (chunk % per_tile) * rows_edge + k
            found += [(tile, row, 0, OFF), (tile, row, side - OFF, OFF)]
        return found

    chunks = tiles * per_tile
    stores = []
    for t in range(tiles):
        for n, part in enumerate(
            (
                piece(t, 1, 0, side, 0),
                piece(t, 1, side - 1, side, 0),
                piece(t, side - 2, 1, OFF, 0),
                piece(t, side - 2, 1, OFF, side - OFF),
            )
        ):
            stores.append(
                pltpu.make_async_copy(out_ref.at[part], out_hbm.at[part], store_sem.at[t, n])
            )
    do_conv(caps, buf_b)
    do_mlp(caps, buf_b)
    do_conv(sides(0), buf_a)

    @pl.loop(0, chunks // 2 - 1)
    def _(i):
        do_mlp(sides(2 * i), buf_a)
        do_conv(sides(2 * i + 1), buf_b)
        do_mlp(sides(2 * i + 1), buf_b)
        do_conv(sides(2 * i + 2), buf_a)

    do_mlp(sides(chunks - 2), buf_a)
    do_conv(sides(chunks - 1), buf_b)
    do_mlp(sides(chunks - 1), buf_b)
    for copy in stores:
        copy.start()
    for copy in inner_copies + stores:
        copy.wait()


def per_device(
    sizes,
    cells,
    partner_edge,
    edge_flip,
    dw_weight,
    dw_bias,
    ln_gain,
    ln_bias,
    w_in,
    b_in,
    w_out,
    b_out,
    layer_scale,
):
    tiles, side, _, channels = cells.shape
    hidden = w_in.shape[0]
    edges = 4 * tiles
    vmem = pl.BlockSpec(memory_space=pltpu.VMEM)
    smem = pl.BlockSpec(memory_space=pltpu.SMEM)
    anywhere = pl.BlockSpec(memory_space=pltpu.HBM)
    dw_bias, ln_gain, ln_bias, b_out, layer_scale = (
        vector.reshape(1, channels)
        for vector in (dw_bias, ln_gain, ln_bias, b_out, layer_scale)
    )
    pad_shape = (tiles * (side + 2), side + 2 * OFF, channels)
    buffers = [pltpu.VMEM((CELLS_PER_CHUNK, 2 * channels), jnp.bfloat16)] * 2
    inner, pad, rims, recv, w_aug = pl.pallas_call(
        functools.partial(inner_kernel, sizes),
        out_shape=(
            pltpu.VMEM(cells.shape, jnp.bfloat16),
            pltpu.VMEM(pad_shape, jnp.float32),
            pltpu.VMEM((edges, side, channels), jnp.bfloat16),
            pltpu.VMEM((2 * CROSS, side, channels), jnp.bfloat16),
            pltpu.VMEM((2 * channels, hidden), jnp.bfloat16),
        ),
        in_specs=[smem, anywhere] + [vmem] * 9,
        out_specs=(vmem,) * 5,
        scratch_shapes=[
            pltpu.VMEM(cells.shape, jnp.bfloat16),
            pltpu.VMEM((2 * CROSS, side, channels), jnp.bfloat16),
            *buffers,
            pltpu.SemaphoreType.DMA((tiles,)),
            pltpu.SemaphoreType.DMA((2,)),
            pltpu.SemaphoreType.DMA((2,)),
        ],
        compiler_params=pltpu.CompilerParams(
            collective_id=0, has_side_effects=True, vmem_limit_bytes=GRANT
        ),
        name="inner",
    )(
        partner_edge,
        cells,
        dw_weight,
        dw_bias,
        ln_gain,
        ln_bias,
        w_in,
        b_in,
        w_out,
        b_out,
        layer_scale,
    )
    return pl.pallas_call(
        functools.partial(edge_kernel, sizes),
        out_shape=(
            jax.ShapeDtypeStruct(cells.shape, jnp.bfloat16),
            pltpu.VMEM(pad_shape, jnp.float32),
        ),
        in_specs=[smem, smem] + [vmem] * 12,
        out_specs=(anywhere, vmem),
        input_output_aliases={3: 1},
        scratch_shapes=[
            pltpu.VMEM(cells.shape, jnp.bfloat16),
            *buffers,
            pltpu.SemaphoreType.DMA((tiles,)),
            pltpu.SemaphoreType.DMA((tiles, 4)),
        ],
        compiler_params=pltpu.CompilerParams(vmem_limit_bytes=GRANT),
        name="edge",
    )(
        partner_edge,
        edge_flip,
        inner,
        pad,
        rims,
        recv,
        w_aug,
        dw_weight,
        dw_bias,
        ln_gain,
        ln_bias,
        w_out,
        b_out,
        layer_scale,
    )[0]


def solution(mesh):
    spread_spec = P(AXES, None, None, None)
    in_specs = (spread_spec, P(AXES, None), P(AXES, None)) + (P(),) * 9
    sizes = (mesh.shape["tile"], mesh.shape["hidden"])
    return jax.shard_map(
        functools.partial(per_device, sizes),
        mesh=mesh,
        in_specs=in_specs,
        out_specs=spread_spec,
        check_vma=False,
    )
```

time: 25 us -> 30.8 us (1.23)
  local copies, waits for them, and re-layouts: 3.48 us -> 8.82 us
    unnamed x1 -> x24, local copies, waits for them, and re-layouts: 3.48 us -> 8.82 us
    pallas_call x1 -> x2, Pallas kernels: 21.4 us -> 21.6 us  [the longest x1 14.9 us: per_device(): pl.pallas_call(functools.partial(inner_kernel, sizes), out_shape=(pltpu.V...]
where the time goes in v3:
time: 30.8 us; the launch traced here: 30.5 us
  Pallas kernels  21.6 us (70%)
  local copies, waits for them, and re-layouts  8.82 us (29%)
    pallas_call x1, Pallas kernels, per_device(): pl.pallas_call(functools.partial(inner_kernel, sizes), out_shape=(pltpu.V...  14.9 us
    unnamed x24, local copies, waits for them, and re-layouts  8.82 us
    pallas_call x1, Pallas kernels, per_device(): pl.pallas_call(functools.partial(edge_kernel, sizes), out_shape=(jax.Shap...  6.75 us

profile of v3, /device:TPU:0, one launch (start us, length us, event | category | flops | bytes accessed | tf_op | source)
XLA Modules:
  0.0 30.5 jit_solution(4921485167010955119)
XLA Ops:
  0.0 0.0 copy-start.5
  0.0 0.0 copy-start
  0.0 1.7 %copy-done = bf16[4,48,48,128]{3,2,1,0:T(8,128)(2,1)S(1)} copy-done((bf16[4,48,48,128]{3,2,1,0:T(8,128)(2,1)S(1)}, bf16[4,48,48,128]{3,2,1,0:T(8,128)(2,1)}, u32[]{:S(2)}) %copy-start) | copy-done | bytes 2359320
  1.7 0.0 copy-start.1
  1.7 0.9 %copy-done.1 = bf16[512,128]{1,0:T(8,128)(2,1)S(1)} copy-done((bf16[512,128]{1,0:T(8,128)(2,1)S(1)}, bf16[512,128]{1,0:T(8,128)(2,1)}, u32[]{:S(2)}) %copy-start.1) | copy-done | bytes 131096
  2.6 0.0 copy-start.2
  2.6 0.9 %copy-done.2 = bf16[512,128]{1,0:T(8,128)(2,1)S(1)} copy-done((bf16[512,128]{1,0:T(8,128)(2,1)S(1)}, bf16[512,128]{1,0:T(8,128)(2,1)}, u32[]{:S(2)}) %copy-start.2) | copy-done | bytes 131096
  3.5 0.0 copy-start.3
  3.5 0.7 %copy-done.3 = f32[9,128]{1,0:T(8,128)S(1)} copy-done((f32[9,128]{1,0:T(8,128)S(1)}, f32[9,128]{1,0:T(8,128)}, u32[]{:S(2)}) %copy-start.3) | copy-done | bytes 4632
  4.2 0.0 copy-start.4
  4.2 0.7 %copy-done.4 = s32[4,4]{1,0:T(4,128)S(1)} copy-done((s32[4,4]{1,0:T(4,128)S(1)}, s32[4,4]{1,0:T(4,128)}, u32[]{:S(2)}) %copy-start.4) | copy-done | bytes 88
  4.9 0.0 copy-start.6
  4.9 0.7 %copy-done.6 = f32[128]{0:T(128)S(1)} copy-done((f32[128]{0:T(128)S(1)}, f32[128]{0:T(128)}, u32[]{:S(2)}) %copy-start.6) | copy-done | bytes 536
  5.5 0.0 copy-start.7
  5.5 0.7 %copy-done.7 = f32[128]{0:T(128)S(1)} copy-done((f32[128]{0:T(128)S(1)}, f32[128]{0:T(128)}, u32[]{:S(2)}) %copy-start.7) | copy-done | bytes 536
  6.2 0.0 copy-start.8
  6.2 0.7 %copy-done.8 = f32[128]{0:T(128)S(1)} copy-done((f32[128]{0:T(128)S(1)}, f32[128]{0:T(128)}, u32[]{:S(2)}) %copy-start.8) | copy-done | bytes 536
  6.8 0.0 copy-start.9
  6.8 0.7 %copy-done.9 = f32[128]{0:T(128)S(1)} copy-done((f32[128]{0:T(128)S(1)}, f32[128]{0:T(128)}, u32[]{:S(2)}) %copy-start.9) | copy-done | bytes 536
  7.5 0.0 copy-start.10
  7.5 0.7 %copy-done.10 = f32[128]{0:T(128)S(1)} copy-done((f32[128]{0:T(128)S(1)}, f32[128]{0:T(128)}, u32[]{:S(2)}) %copy-start.10) | copy-done | bytes 536
  8.2 0.0 copy-start.11
  8.2 0.7 %copy-done.11 = bf16[512]{0:T(512)(128)(2,1)S(1)} copy-done((bf16[512]{0:T(512)(128)(2,1)S(1)}, bf16[512]{0:T(512)(128)(2,1)}, u32[]{:S(2)}) %copy-start.11) | copy-done | bytes 1048
  8.8 14.9 %inner.1 = (bf16[4,48,48,128]{3,2,1,0:T(8,128)(2,1)S(1)}, f32[200,64,128]{2,1,0:T(8,128)S(1)}, bf16[16,48,128]{2,1,0:T(8,128)(2,1)S(1)}, bf16[8,48,128]{2,1,0:T(8,128)(2,1)S(1)}, bf16[256,512]{1,0:T(8,128)(2,1)S(1)}) custom-call(s32[4,4]{1,0:T(4,128)S(1)} %copy-done.4, bf16[4,48,48,128]{3,2,1,0:T(8,128)(2,1)S(1)} %copy-done, f32[9,128]{1,0:T(8,128)S(1)} %copy-done.3, ...), custom_call_target="tpu_custom_call" | custom-call | tf_op jit(solution)/shard_map/inner/pallas_call | solution.py:395
  23.7 0.0 copy-done.5
  23.7 6.7 %edge.1 = (bf16[4,48,48,128]{3,2,1,0:T(8,128)(2,1)}, f32[200,64,128]{2,1,0:T(8,128)S(1)}) custom-call(s32[4,4]{1,0:T(4,128)S(1)} %copy-done.4, s32[4,4]{1,0:T(4,128)S(1)} %copy-done.5, bf16[4,48,48,128]{3,2,1,0:T(8,128)(2,1)S(1)} %get-tuple-element.11.inner_ref, f32[200,64,128]{2,1,0:T(8,128)S(1)} %get-tuple-element.12.pad_in_ref, ...), custom_call_target="tpu_custom_call", output_to_operand_aliasing={{1}: (3, {})} | custom-call | tf_op jit(solution)/shard_map/edge/pallas_call | solution.py:431
Async XLA Ops:
  0.0 23.7 %copy-start.5 = (s32[4,4]{1,0:T(4,128)S(1)}, s32[4,4]{1,0:T(4,128)}, u32[]{:S(2)}) copy-start(s32[4,4]{1,0:T(4,128)} %flip_ref.1) | copy-start | bytes 196
  0.0 1.7 %copy-start = (bf16[4,48,48,128]{3,2,1,0:T(8,128)(2,1)S(1)}, bf16[4,48,48,128]{3,2,1,0:T(8,128)(2,1)}, u32[]{:S(2)}) copy-start(bf16[4,48,48,128]{3,2,1,0:T(8,128)(2,1)} %cells_ref.1) | copy-start | bytes 7077892
  1.7 0.9 %copy-start.1 = (bf16[512,128]{1,0:T(8,128)(2,1)S(1)}, bf16[512,128]{1,0:T(8,128)(2,1)}, u32[]{:S(2)}) copy-start(bf16[512,128]{1,0:T(8,128)(2,1)} %w_out_ref.3) | copy-start | bytes 393220
  2.6 0.9 %copy-start.2 = (bf16[512,128]{1,0:T(8,128)(2,1)S(1)}, bf16[512,128]{1,0:T(8,128)(2,1)}, u32[]{:S(2)}) copy-start(bf16[512,128]{1,0:T(8,128)(2,1)} %w_in_ref.1) | copy-start | bytes 393220
  3.5 0.7 %copy-start.3 = (f32[9,128]{1,0:T(8,128)S(1)}, f32[9,128]{1,0:T(8,128)}, u32[]{:S(2)}) copy-start(f32[9,128]{1,0:T(8,128)} %dw_ref.3) | copy-start | bytes 13828
  4.2 0.7 %copy-start.4 = (s32[4,4]{1,0:T(4,128)S(1)}, s32[4,4]{1,0:T(4,128)}, u32[]{:S(2)}) copy-start(s32[4,4]{1,0:T(4,128)} %partner_ref.3) | copy-start | bytes 196
  4.9 0.7 %copy-start.6 = (f32[128]{0:T(128)S(1)}, f32[128]{0:T(128)}, u32[]{:S(2)}) copy-start(f32[128]{0:T(128)} %param.16) | copy-start | bytes 1540
  5.5 0.7 %copy-start.7 = (f32[128]{0:T(128)S(1)}, f32[128]{0:T(128)}, u32[]{:S(2)}) copy-start(f32[128]{0:T(128)} %param.17) | copy-start | bytes 1540
  6.2 0.7 %copy-start.8 = (f32[128]{0:T(128)S(1)}, f32[128]{0:T(128)}, u32[]{:S(2)}) copy-start(f32[128]{0:T(128)} %param.18) | copy-start | bytes 1540
  6.8 0.7 %copy-start.9 = (f32[128]{0:T(128)S(1)}, f32[128]{0:T(128)}, u32[]{:S(2)}) copy-start(f32[128]{0:T(128)} %param.22) | copy-start | bytes 1540
  7.5 0.7 %copy-start.10 = (f32[128]{0:T(128)S(1)}, f32[128]{0:T(128)}, u32[]{:S(2)}) copy-start(f32[128]{0:T(128)} %param.23) | copy-start | bytes 1540
  8.2 0.7 %copy-start.11 = (bf16[512]{0:T(512)(128)(2,1)S(1)}, bf16[512]{0:T(512)(128)(2,1)}, u32[]{:S(2)}) copy-start(bf16[512]{0:T(512)(128)(2,1)} %b_in_ref.1) | copy-start | bytes 3076

commit v4 on v3

--- a/solution.py
+++ b/solution.py
@@ -389,6 +389,36 @@
     dw_bias, ln_gain, ln_bias, b_out, layer_scale = (
         vector.reshape(1, channels)
         for vector in (dw_bias, ln_gain, ln_bias, b_out, layer_scale)
+    )
+    (
+        cells,
+        partner_edge,
+        edge_flip,
+        dw_weight,
+        dw_bias,
+        ln_gain,
+        ln_bias,
+        w_in,
+        b_in,
+        w_out,
+        b_out,
+        layer_scale,
+    ) = (
+        pltpu.with_memory_space_constraint(array, pltpu.HBM)
+        for array in (
+            cells,
+            partner_edge,
+            edge_flip,
+            dw_weight,
+            dw_bias,
+            ln_gain,
+            ln_bias,
+            w_in,
+            b_in,
+            w_out,
+            b_out,
+            layer_scale,
+        )
     )
     pad_shape = (tiles * (side + 2), side + 2 * OFF, channels)
     buffers = [pltpu.VMEM((CELLS_PER_CHUNK, 2 * channels), jnp.bfloat16)] * 2

time: 30.8 us -> 21.8 us (0.71)
  local copies, waits for them, and re-layouts: 8.82 us -> 0 us
    unnamed x24 -> x0, local copies, waits for them, and re-layouts: 8.82 us -> none
    pallas_call x1, Pallas kernels: 14.9 us -> 14.5 us  [per_device(): pl.pallas_call(functools.partial(inner_kernel, sizes), out_shape=(pltpu.V...]
where the time goes in v4:
time: 21.8 us; the launch traced here: 21.6 us
  Pallas kernels  21.6 us (99%)
    pallas_call x1, Pallas kernels, per_device(): pl.pallas_call(functools.partial(inner_kernel, sizes), out_shape=(pltpu.V...  14.5 us
    pallas_call x1, Pallas kernels, per_device(): pl.pallas_call(functools.partial(edge_kernel, sizes), out_shape=(jax.Shap...  7.06 us

profile of v4, /device:TPU:0, one launch (start us, length us, event | category | flops | bytes accessed | tf_op | source)
XLA Modules:
  0.0 21.6 jit_solution(700578718321727846)
XLA Ops:
  0.0 14.5 %inner.1 = (bf16[4,48,48,128]{3,2,1,0:T(8,128)(2,1)S(1)}, f32[200,64,128]{2,1,0:T(8,128)S(1)}, bf16[16,48,128]{2,1,0:T(8,128)(2,1)S(1)}, bf16[8,48,128]{2,1,0:T(8,128)(2,1)S(1)}, bf16[256,512]{1,0:T(8,128)(2,1)S(1)}) custom-call(s32[4,4]{1,0:T(4,128)} %partner_ref.3, bf16[4,48,48,128]{3,2,1,0:T(8,128)(2,1)} %cells_ref.1, f32[9,128]{1,0:T(8,128)} %dw_ref.3, ...), custom_call_target="tpu_custom_call" | custom-call | tf_op jit(solution)/shard_map/inner/pallas_call | solution.py:425
  14.5 7.1 %edge.1 = (bf16[4,48,48,128]{3,2,1,0:T(8,128)(2,1)}, f32[200,64,128]{2,1,0:T(8,128)S(1)}) custom-call(s32[4,4]{1,0:T(4,128)} %partner_ref.3, s32[4,4]{1,0:T(4,128)} %flip_ref.1, bf16[4,48,48,128]{3,2,1,0:T(8,128)(2,1)S(1)} %get-tuple-element.11.inner_ref, f32[200,64,128]{2,1,0:T(8,128)S(1)} %get-tuple-element.12.pad_in_ref, ...), custom_call_target="tpu_custom_call", output_to_operand_aliasing={{1}: (3, {})} | custom-call | tf_op jit(solution)/shard_map/edge/pallas_call | solution.py:461
